TPU v7x, 32 devices: a whole 2x2x4 slice. The times are simulated.
32 devices in a mesh: groups: 2 (over y), wide: 4 (over z), narrow: 4 (over x, core).
Axes of the slice: x: 2, y: 2, z: 4, core: 2. Of those that a mesh axis runs over, the one named last changes fastest.
Arguments:
- residual: bfloat16 [512, 4096], P(('groups', 'wide')), parts along dimension 0, may hold values from -6 to 6
- query_rows: bfloat16 [512, 4096], P(('groups', 'wide'), 'narrow'), parts along dimension 0, may hold values from -160 to 160
- key_rows: bfloat16 [512, 4096], P(('groups', 'wide'), 'narrow'), parts along dimension 0, may hold values from -160 to 160
- value_rows: bfloat16 [512, 4096], P(('groups', 'wide'), 'narrow'), parts along dimension 0, may hold values from -6 to 6
- segment_ids: int32 [8, 64], P(('groups', 'wide')), parts along dimension 0, may hold values from 0 to 3, never falling along the last dimension, each value on 1 to 32 neighbouring positions
- o_weight: bfloat16 [4096, 4096], P('narrow', 'wide'), may hold values from -0.09375 to 0.09375
- norm_gain: float32 [4096], replicated, may hold values from 0.1 to 1.9
- w_gate: bfloat16 [32, 4096, 1024], P('wide', None, 'narrow'), may hold values from -0.09375 to 0.09375
- w_up: bfloat16 [32, 4096, 1024], P('wide', None, 'narrow'), may hold values from -0.09375 to 0.09375
- w_down: bfloat16 [32, 1024, 4096], P('wide', None, 'narrow'), may hold values from -0.1875 to 0.1875
- expert_ids: int32 [512, 8], P(('groups', 'wide')), parts along dimension 0, may hold values from 0 to 31, all different within a row; in each aligned block of 16 rows (0 to 15, 16 to 31, ...) at most 8 rows name the same one
- gate_weights: float32 [512, 8], P(('groups', 'wide')), parts along dimension 0, may hold values from 0.05 to 1
- target: bfloat16 [512, 4096], P(('groups', 'wide', 'narrow')), parts along dimension 0, may hold values from -6 to 6
Outputs:
- errors: float32 [512], P(('groups', 'wide', 'narrow')), parts along dimension 0
There are 2 independent parts, one for each index of `groups`. A program takes and returns all parts, laid end to end along the dimension named above; an argument that names none is the same for every part. Nothing has to cross between parts.
Inputs may be any that keep to these rules, and one draw needn't show every extreme that they name: `expert_ids`: in each aligned block of 16 rows (the rows of one device) no expert is named more than 8 times, a bound that some block reaches. `segment_ids`: along each row the trajectory number never falls; a trajectory covers 1 to 32 positions.
All inputs are finite; a program needn't handle non-finite values.
Results may differ from a plain program's by a relative error of at most 0.0005.
Values may be sent and summed in bfloat16 or wider, within the bound.
No kernel may reach another device: no remote copies, remote signals or barrier semaphores. Data moves between devices by JAX's collectives and lax.ppermute only.
A program may use at most 128 MiB of HBM per device.

v0:
```python
import jax
import jax.numpy as jnp
from jax import lax
from jax.sharding import PartitionSpec as P

HD = 128
EXPERTS = 32
TOP = 8


def attend(query_block, key_block, value_block, seg_row):
    tok_count = query_block.shape[0]
    head_count = query_block.shape[1] // HD
    query_heads = query_block.reshape(tok_count, head_count, HD)
    key_heads = key_block.reshape(tok_count, head_count, HD)
    value_heads = value_block.reshape(tok_count, head_count, HD)
    scores = jnp.einsum(
        "qhd,khd->hqk", query_heads, key_heads, preferred_element_type=jnp.float32
    ) * HD ** (-0.5)
    places = jnp.arange(tok_count, dtype=jnp.int32)
    allowed = (seg_row[:, None] == seg_row[None, :]) & (places[None, :] <= places[:, None])
    scores = jnp.where(allowed[None], scores, -jnp.inf)
    peak_score = jnp.max(scores, axis=2, keepdims=True)
    weights = jnp.exp(scores - peak_score)
    denom_sum = jnp.sum(weights, axis=2, keepdims=True)
    mixed_out = jnp.einsum(
        "hqk,khd->qhd",
        weights.astype(jnp.bfloat16),
        value_heads,
        preferred_element_type=jnp.float32,
    )
    mixed_out = mixed_out / jnp.transpose(denom_sum, (1, 0, 2))
    return mixed_out.reshape(tok_count, -1).astype(jnp.bfloat16)


def normalize(stream_rows, gain_vector):
    mean_sq = jnp.mean(stream_rows * stream_rows, axis=1, keepdims=True)
    return (stream_rows * lax.rsqrt(mean_sq + 1e-06) * gain_vector).astype(jnp.bfloat16)


def slot_positions(expert_list):
    row_count, route_count = expert_list.shape
    flat_ids = expert_list.reshape(-1)
    onehot = (flat_ids[:, None] == jnp.arange(EXPERTS, dtype=jnp.int32)[None, :]).astype(jnp.int32)
    before = jnp.cumsum(onehot, axis=0) - onehot
    return jnp.sum(before * onehot, axis=1).reshape(row_count, route_count)


def fill_slots(row_data, slot_index, row_index, slot_total):
    source = (
        jnp.full((slot_total,), -1, jnp.int32).at[slot_index.reshape(-1)].set(row_index.reshape(-1))
    )
    picked = row_data[jnp.maximum(source, 0)]
    return jnp.where((source >= 0)[:, None], picked, jnp.zeros((), row_data.dtype))


def body(
    residual,
    query_rows,
    key_rows,
    value_rows,
    segment_ids,
    o_weight,
    norm_gain,
    w_gate,
    w_up,
    w_down,
    expert_ids,
    gate_weights,
    target,
):
    wide_count = lax.axis_size("wide")
    narrow_count = lax.axis_size("narrow")
    narrow_here = lax.axis_index("narrow")
    tok_count = query_rows.shape[0]
    row_count = tok_count // narrow_count
    capacity = max(2, 2 * row_count * TOP // EXPERTS)
    local_experts = w_gate.shape[0]
    model_width = residual.shape[1]
    attended = attend(query_rows, key_rows, value_rows, segment_ids[0])
    partial_mix = jnp.dot(
        attended,
        lax.all_gather(o_weight, "wide", axis=1, tiled=True),
        preferred_element_type=jnp.float32,
    )
    own_ids = lax.dynamic_slice_in_dim(expert_ids, narrow_here * row_count, row_count, 0)
    own_gates = lax.dynamic_slice_in_dim(gate_weights, narrow_here * row_count, row_count, 0)
    mixed_own = lax.psum_scatter(partial_mix, "narrow", scatter_dimension=0, tiled=True)
    own_resid = lax.dynamic_slice_in_dim(residual, narrow_here * row_count, row_count, 0)
    stream = own_resid.astype(jnp.float32) + mixed_own
    normed_own = normalize(stream, norm_gain)
    own_pos = slot_positions(own_ids)
    slot_index = own_ids * capacity + own_pos
    row_index = jnp.broadcast_to(jnp.arange(row_count, dtype=jnp.int32)[:, None], own_ids.shape)
    outgoing = fill_slots(normed_own, slot_index, row_index, EXPERTS * capacity)
    incoming = lax.all_to_all(
        outgoing.reshape(wide_count, -1, model_width),
        "wide",
        split_axis=0,
        concat_axis=0,
        tiled=True,
    )
    incoming = incoming.reshape(wide_count, local_experts, 1, capacity, model_width)
    grouped = lax.all_gather(incoming, "narrow", axis=2, tiled=True)
    expert_rows = grouped.reshape(wide_count, local_experts, narrow_count * capacity, model_width)
    gate_val = jnp.einsum("wesd,edh->wesh", expert_rows, w_gate, preferred_element_type=jnp.float32)
    up_val = jnp.einsum("wesd,edh->wesh", expert_rows, w_up, preferred_element_type=jnp.float32)
    hidden = (jax.nn.silu(gate_val) * up_val).astype(jnp.bfloat16)
    slice_width = w_down.shape[2]
    outcome = jnp.einsum(
        "wesh,ehd->wesd",
        lax.all_gather(hidden, "narrow", axis=3, tiled=True),
        w_down,
        preferred_element_type=jnp.float32,
    ).astype(jnp.bfloat16)
    outcome = outcome.reshape(wide_count, local_experts, narrow_count, capacity, slice_width)
    returned = lax.all_to_all(
        lax.all_to_all(outcome, "wide", split_axis=0, concat_axis=0, tiled=True),
        "narrow",
        split_axis=2,
        concat_axis=4,
        tiled=True,
    )
    returned = returned.reshape(EXPERTS * capacity, model_width)
    chosen = returned[own_ids * capacity + own_pos]
    moe_sum = jnp.sum(own_gates[:, :, None] * chosen.astype(jnp.float32), axis=1)
    predicted = stream + moe_sum
    return jnp.mean((predicted - target.astype(jnp.float32)) ** 2, axis=1)


def solution(mesh):
    return jax.shard_map(
        body,
        mesh=mesh,
        in_specs=(
            P(("groups", "wide"), None),
            P(("groups", "wide"), "narrow"),
            P(("groups", "wide"), "narrow"),
            P(("groups", "wide"), "narrow"),
            P(("groups", "wide"), None),
            P("narrow", "wide"),
            P(),
            P("wide", None, "narrow"),
            P("wide", None, "narrow"),
            P("wide", None, "narrow"),
            P(("groups", "wide"), None),
            P(("groups", "wide"), None),
            P(("groups", "wide", "narrow"), None),
        ),
        out_specs=P(("groups", "wide", "narrow")),
        check_vma=False,
    )
```

profile of v0, /device:TPU:0, one launch (start us, length us, event | category | flops | bytes accessed | tf_op | source)
XLA Modules:
  0.0 455.0 jit_solution(6789663493847794399)
XLA Ops:
  6.5 0.7 all-gather.4.cloned.1.call-update
  7.3 0.0 reduce-scatter.2.cloned.1.call-start
  7.3 0.8 fusion.51
  8.1 1.2 fusion.55
  9.3 0.1 fusion.37
  9.4 0.2 fusion.36
  9.7 151.6 %all-gather.4.cloned.1.call-done = bf16[1024,4096]{1,0:T(8,128)(2,1)} async-done(((bf16[1024,1024]{1,0:T(8,128)(2,1)}), bf16[1024,4096]{1,0:T(8,128)(2,1)}) %all-gather.4.cloned.1.call-update) | async-done | bytes 8388624 | tf_op jit(solution)/shard_map/all_gather | solution.py:83
  161.3 6.0 %fusion.40 = f32[64,4096]{1,0:T(8,128)} fusion(bf16[1024,4096]{1,0:T(8,128)(2,1)} %all-gather.4.cloned.1.call-done, bf16[8,8,8,128]{3,2,1,0:T(8,128)(2,1)S(1)} %fusion.36), kind=kOutput, calls=%fused_computation.34 | convolution fusion | flops 536870912 | bytes 9568256 | tf_op jit(solution)/shard_map/dot_general | solution.py:81
  167.3 0.0 reduce-scatter.2.cloned.1.call-update
  167.3 0.0 all-gather.6.cloned.1.call-start
  167.4 0.1 constant_dynamic-slice_fusion
  167.5 0.1 copy.45
  167.5 0.1 eq.38
  167.6 0.1 fusion.50
  167.7 0.2 reduce_window_sum.11
  167.9 0.2 select_reduce_fusion
  168.1 0.1 reshape.127
  168.2 0.1 reshape.128
  168.3 0.1 reshape.154
  168.4 1.0 scatter_custom_fusion
  169.4 0.1 broadcast_in_dim.59
  169.5 21.0 %reduce-scatter.2.cloned.1.call-done = f32[16,4096]{1,0:T(8,128)} async-done(((f32[64,4096]{1,0:T(8,128)}), f32[16,4096]{1,0:T(8,128)}) %reduce-scatter.2.cloned.1.call-update) | async-done | bytes 262160 | tf_op jit(solution)/shard_map/reduce_scatter | solution.py:88
  190.5 1.1 multiply_reduce_fusion.1
  191.6 1.0 multiply_convert_fusion
  192.6 1.8 gather_fusion
  194.5 0.2 broadcast_select_fusion
  194.7 52.5 %all_to_all.25 = bf16[4,64,4096]{2,1,0:T(8,128)(2,1)} all-to-all(bf16[4,64,4096]{2,1,0:T(8,128)(2,1)S(1)} %broadcast_select_fusion), channel_id=1, replica_groups=mesh['groups'=2,'wide'=4,'narrow'=4] {'wide'}, dimensions={0} | all-to-all | bytes 4194304 | tf_op jit(solution)/shard_map/all_to_all | solution.py:96
  247.2 0.0 all-gather.6.cloned.1.call-update
  247.3 0.2 all-gather.8.cloned.1.call-start
  247.5 56.3 %all-gather.6.cloned.1.call-done = bf16[4,8,4,8,4096]{4,3,1,0,2:T(8,128)(2,1)} async-done(((bf16[4,8,1,8,4096]{4,3,1,0,2:T(8,128)(2,1)}), bf16[4,8,4,8,4096]{4,3,1,0,2:T(8,128)(2,1)}) %all-gather.6.cloned.1.call-update) | async-done | bytes 8388624 | tf_op jit(solution)/shard_map/all_gather | solution.py:104
  303.8 10.5 %fusion.13 = f32[4,8,32,256]{3,2,0,1:T(8,128)S(1)} fusion(bf16[8,4096,256]{2,1,0:T(8,128)(2,1)} %param.20, bf16[4,8,4,8,4096]{4,3,1,0,2:T(8,128)(2,1)} %all-gather.6.cloned.1.call-done), kind=kOutput, calls=%fused_computation.17 | convolution fusion | flops 2147483648 | bytes 26214400 | tf_op jit(solution)/shard_map/wesd,edh->wesh/dot_general | solution.py:106
  314.3 11.5 %fusion.28 = bf16[4,8,32,256]{3,2,0,1:T(8,128)(2,1)} fusion(bf16[8,4096,256]{2,1,0:T(8,128)(2,1)} %param.21, bf16[4,8,4,8,4096]{4,3,1,0,2:T(8,128)(2,1)} %all-gather.6.cloned.1.call-done, f32[4,8,32,256]{3,2,0,1:T(8,128)S(1)} %fusion.13), kind=kOutput, calls=%fused_computation.20 | convolution fusion | flops 2149056512 | bytes 26738688 | tf_op jit(solution)/shard_map/wesd,edh->wesh/dot_general | solution.py:107
  325.8 23.0 %all-gather.8.cloned.1.call-done = bf16[4,8,32,1024]{3,2,0,1:T(8,128)(2,1)} async-done(((bf16[4,8,32,256]{3,2,0,1:T(8,128)(2,1)}), bf16[4,8,32,1024]{3,2,0,1:T(8,128)(2,1)}) %all-gather.8.cloned.1.call-update) | async-done | bytes 2097168 | tf_op jit(solution)/shard_map/all_gather | solution.py:112
  348.8 8.8 %convert_bitcast_fusion = bf16[4,8,4,8,1024]{4,3,2,0,1:T(8,128)(2,1)S(1)} fusion(bf16[4,8,32,1024]{3,2,0,1:T(8,128)(2,1)} %all-gather.8.cloned.1.call-done, bf16[8,1024,1024]{2,1,0:T(8,128)(2,1)} %param.22), kind=kOutput, calls=%fused_computation.15 | convolution fusion | flops 2148532224 | bytes 20971520 | tf_op jit(solution)/shard_map/wesh,ehd->wesd/dot_general | solution.py:110
  357.6 0.2 copy.38
  357.8 53.0 %all_to_all.26 = bf16[4,8,4,8,1024]{4,3,2,1,0:T(8,128)(2,1)S(1)} all-to-all(bf16[4,8,4,8,1024]{4,3,2,1,0:T(8,128)(2,1)S(1)} %copy.38), channel_id=1, replica_groups=mesh['groups'=2,'wide'=4,'narrow'=4] {'wide'}, dimensions={0} | all-to-all | bytes 4194304 | tf_op jit(solution)/shard_map/all_to_all | solution.py:118
  410.8 1.5 copy.39
  412.3 3.6 all-to-all-start.2
  415.9 0.1 reshape.144
  416.0 0.1 constant_dynamic-slice_fusion.1
  416.1 0.1 copy.35
  416.2 25.4 %all-to-all-done.2 = bf16[4,8,4,8,1024]{4,3,0,1,2:T(8,128)(2,1)S(1)} async-done(((bf16[4,8,4,8,1024]{4,3,0,1,2:T(8,128)(2,1)}), bf16[4,8,4,8,1024]{4,3,0,1,2:T(8,128)(2,1)S(1)}, u32[]{:S(2)}, u32[]{:S(2)}) %all-to-all-start.2) | async-done | bytes 2097184 | tf_op jit(solution)/shard_map/all_to_all | solution.py:117
  441.5 1.3 copy-done.2
  442.9 1.8 copy.40
  444.7 1.2 gather_fusion.1
  445.9 0.8 fusion.10
  446.7 1.2 multiply_reduce_fusion
  447.9 0.5 broadcast_multiply_fusion
  (25 shorter events, 0.1 us)
Async XLA Ops:
  6.5 2.8 copy-start
  6.5 154.7 %all-gather.4.cloned.1.call-start = ((), (), s32[]{:S(2)}) async-start(), calls=%async_computation.4 | async-start | bytes 10485760 | tf_op jit(solution)/shard_map/all_gather | solution.py:83
  7.3 183.2 %reduce-scatter.2.cloned.1.call-start = ((), (), s32[]{:S(2)}) async-start(), calls=%async_computation.5 | async-start | bytes 1310720 | tf_op jit(solution)/shard_map/reduce_scatter | solution.py:88
  9.6 157.7 %copy-start.6 = (s32[64,8]{0,1:T(8,128)S(1)}, s32[64,8]{0,1:T(8,128)}, u32[]{:S(2)}) copy-start(s32[64,8]{0,1:T(8,128)} %param.23) | copy-start | bytes 6148
  9.6 180.8 %copy-start.4 = (bf16[64,4096]{1,0:T(8,128)(2,1)S(1)}, bf16[64,4096]{1,0:T(8,128)(2,1)}, u32[]{:S(2)}) copy-start(bf16[64,4096]{1,0:T(8,128)(2,1)} %param.13) | copy-start | bytes 1572868
  9.7 181.9 %copy-start.5 = (f32[4096]{0:T(1024)S(1)}, f32[4096]{0:T(1024)}, u32[]{:S(2)}) copy-start(f32[4096]{0:T(1024)} %param.19) | copy-start | bytes 49156
  167.3 136.5 %all-gather.6.cloned.1.call-start = ((), (), s32[]{:S(2)}) async-start(), calls=%async_computation.6 | async-start | bytes 10485760 | tf_op jit(solution)/shard_map/all_gather | solution.py:104
  247.3 101.5 %all-gather.8.cloned.1.call-start = ((), (), s32[]{:S(2)}) async-start(), calls=%async_computation.7 | async-start | bytes 2621440 | tf_op jit(solution)/shard_map/all_gather | solution.py:112
  410.8 5.2 %copy-start.7 = (f32[64,8]{0,1:T(8,128)S(1)}, f32[64,8]{0,1:T(8,128)}, u32[]{:S(2)}) copy-start(f32[64,8]{0,1:T(8,128)} %param.24) | copy-start | bytes 6148
  412.3 29.2 %all-to-all-start.2 = ((bf16[4,8,4,8,1024]{4,3,0,1,2:T(8,128)(2,1)}), bf16[4,8,4,8,1024]{4,3,0,1,2:T(8,128)(2,1)S(1)}, u32[]{:S(2)}, u32[]{:S(2)}) async-start(bf16[4,8,4,8,1024]{4,3,0,1,2:T(8,128)(2,1)} %copy.39), calls=%async_computation.3 | async-start | bytes 4194304 | tf_op jit(solution)/shard_map/all_to_all | solution.py:117
  441.5 1.4 copy-start.2
  444.7 3.7 copy-start.1
  444.7 2.0 copy-start.3
Sparse Core Ops, SparseCore 0:
  8.9 152.3 all-gather.3
  167.4 22.9 reduce-scatter.1
  247.4 56.3 all-gather.5
  325.9 22.8 all-gather.7
where the time goes:
time: 455 us
  waiting for transfers between devices  278 us (61%)
  blocking collectives  106 us (23%)
  matrix products  38.2 us (8%)
  between operations  13.4 us (3%)
  local copies, waits for them, and re-layouts  9.75 us (2%)
  other arithmetic  6.17 us (1%)
    all_gather x1, waiting for transfers between devices, body(): lax.all_gather(o_weight, 'wide', axis=1, tiled=True)  152 us
    all_gather x1, waiting for transfers between devices, body(): grouped = lax.all_gather(incoming, 'narrow', axis=2, tiled=True)  56.3 us
    all_to_all x1, blocking collectives, body(): lax.all_to_all(outcome, 'wide', split_axis=0, concat_axis=0, tiled=True)  53 us
    all_to_all x1, blocking collectives, body(): lax.all_to_all(outgoing.reshape(wide_count, -1, model_width), 'wide', spl...  52.5 us
    all_to_all x1, waiting for transfers between devices, body(): lax.all_to_all(lax.all_to_all(outcome, 'wide', split_axis=0, concat_axis=...  25.4 us
    all_gather x1, waiting for transfers between devices, body(): lax.all_gather(hidden, 'narrow', axis=3, tiled=True)  23 us
    reduce_scatter x1, waiting for transfers between devices, body(): lax.psum_scatter(partial_mix, 'narrow', scatter_dimension=0, tiled=True)  21 us
    dot_general x1, matrix products, body(): jnp.einsum('wesd,edh->wesh', expert_rows, w_up, preferred_element_type=jn...  11.5 us
  transfers between devices with their start and end apart: 5, of which 5 were waited for; matrix products, arithmetic and copies ran while one was open for 1% of the time, Pallas kernels for 0%

commit v1 on v0

--- a/solution.py
+++ b/solution.py
@@ -6,6 +6,12 @@
 HD = 128
 EXPERTS = 32
 TOP = 8
+
+
+def in_order(parts, dim):
+    parts = jnp.moveaxis(parts, 0, dim)
+    lengths = parts.shape
+    return parts.reshape(*lengths[:dim], lengths[dim] * lengths[dim + 1], *lengths[dim + 2 :])
 
 
 def attend(query_block, key_block, value_block, seg_row):
@@ -101,7 +107,14 @@
         tiled=True,
     )
     incoming = incoming.reshape(wide_count, local_experts, 1, capacity, model_width)
-    grouped = lax.all_gather(incoming, "narrow", axis=2, tiled=True)
+    size = lax.axis_size("narrow")
+    forward = [(i, (i + 1) % size) for i in range(size)]
+    parts = [incoming]
+    while len(parts) < size:
+        parts.append(lax.ppermute(parts[-1], "narrow", forward))
+    index = lax.axis_index("narrow")
+    parts = jnp.stack(parts)[(index - jnp.arange(size)) % size]
+    grouped = in_order(parts, 2)
     expert_rows = grouped.reshape(wide_count, local_experts, narrow_count * capacity, model_width)
     gate_val = jnp.einsum("wesd,edh->wesh", expert_rows, w_gate, preferred_element_type=jnp.float32)
     up_val = jnp.einsum("wesd,edh->wesh", expert_rows, w_up, preferred_element_type=jnp.float32)

time: 455 us -> 492 us (1.081)
  waiting for transfers between devices: 278 us -> 296 us
  local copies, waits for them, and re-layouts: 9.75 us -> 23.5 us
    ppermute x0 -> x3, waiting for transfers between devices: none -> 76.3 us  [body(): parts.append(lax.ppermute(parts[-1], 'narrow', forward))]
    all_gather x1 -> x0, waiting for transfers between devices: 56.3 us -> none  [body(): grouped = lax.all_gather(incoming, 'narrow', axis=2, tiled=True)]
    gather x0 -> x3, local copies, waits for them, and re-layouts: none -> 13.7 us  [body(): parts = jnp.stack(parts)[(index - jnp.arange(size)) % size]]
  transfers between devices with their start and end apart: 5 -> 7, of which waited for: 5 -> 7; matrix products, arithmetic and copies ran while one was open for 1% -> 1% of each run, Pallas kernels for 0% -> 0%
where the time goes in v1:
time: 492 us
  waiting for transfers between devices  296 us (60%)
  blocking collectives  105 us (21%)
  matrix products  42.4 us (9%)
  local copies, waits for them, and re-layouts  23.5 us (5%)
  between operations  13.4 us (3%)
  other arithmetic  7.29 us (1%)
    all_gather x1, waiting for transfers between devices, body(): lax.all_gather(o_weight, 'wide', axis=1, tiled=True)  152 us
    ppermute x3, waiting for transfers between devices, body(): parts.append(lax.ppermute(parts[-1], 'narrow', forward))  76.3 us
    all_to_all x1, blocking collectives, body(): lax.all_to_all(outcome, 'wide', split_axis=0, concat_axis=0, tiled=True)  53 us
    all_to_all x1, blocking collectives, body(): lax.all_to_all(outgoing.reshape(wide_count, -1, model_width), 'wide', spl...  52.4 us
    all_to_all x1, waiting for transfers between devices, body(): lax.all_to_all(lax.all_to_all(outcome, 'wide', split_axis=0, concat_axis=...  25.4 us
    all_gather x1, waiting for transfers between devices, body(): lax.all_gather(hidden, 'narrow', axis=3, tiled=True)  21.1 us
    reduce_scatter x1, waiting for transfers between devices, body(): lax.psum_scatter(partial_mix, 'narrow', scatter_dimension=0, tiled=True)  21 us
    gather x3, local copies, waits for them, and re-layouts, body(): parts = jnp.stack(parts)[(index - jnp.arange(size)) % size]  13.7 us
  transfers between devices with their start and end apart: 7, of which 7 were waited for; matrix products, arithmetic and copies ran while one was open for 1% of the time, Pallas kernels for 0%

profile of v1, /device:TPU:0, one launch (start us, length us, event | category | flops | bytes accessed | tf_op | source)
XLA Modules:
  0.0 491.8 jit_solution(10833004847604854866)
XLA Ops:
  6.5 0.7 all-gather.3.cloned.1.call-update
  7.3 0.8 fusion.51
  8.1 1.2 fusion.57
  9.4 0.2 fusion.36
  9.7 151.6 %all-gather.3.cloned.1.call-done = bf16[1024,4096]{1,0:T(8,128)(2,1)} async-done(((bf16[1024,1024]{1,0:T(8,128)(2,1)}), bf16[1024,4096]{1,0:T(8,128)(2,1)}) %all-gather.3.cloned.1.call-update) | async-done | bytes 8388624 | tf_op jit(solution)/shard_map/all_gather | solution.py:89
  161.3 6.0 %fusion.40 = f32[64,4096]{1,0:T(8,128)} fusion(bf16[1024,4096]{1,0:T(8,128)(2,1)} %all-gather.3.cloned.1.call-done, bf16[8,8,8,128]{3,2,1,0:T(8,128)(2,1)S(1)} %fusion.36), kind=kOutput, calls=%fused_computation.40 | convolution fusion | flops 536870912 | bytes 9568256 | tf_op jit(solution)/shard_map/dot_general | solution.py:87
  167.4 0.1 constant_dynamic-slice_fusion
  167.5 0.1 copy.49
  167.5 0.1 eq.40
  167.6 0.1 fusion.50
  167.7 0.2 reduce_window_sum.11
  167.9 0.2 select_reduce_fusion
  168.1 0.1 reshape.173
  168.2 0.1 reshape.174
  168.3 0.1 reshape.219
  168.4 1.0 scatter_custom_fusion
  169.4 0.1 broadcast_in_dim.60
  169.5 21.0 %reduce-scatter.2.cloned.1.call-done = f32[16,4096]{1,0:T(8,128)} async-done(((f32[64,4096]{1,0:T(8,128)}), f32[16,4096]{1,0:T(8,128)}) %reduce-scatter.2.cloned.1.call-update) | async-done | bytes 262160 | tf_op jit(solution)/shard_map/reduce_scatter | solution.py:94
  190.5 1.1 multiply_reduce_fusion.1
  191.6 1.0 multiply_convert_fusion
  192.6 1.8 gather_fusion
  194.5 0.2 broadcast_select_fusion
  194.7 52.4 %all_to_all.25 = bf16[4,64,4096]{2,1,0:T(8,128)(2,1)S(1)} all-to-all(bf16[4,64,4096]{2,1,0:T(8,128)(2,1)S(1)} %broadcast_select_fusion), channel_id=1, replica_groups=mesh['groups'=2,'wide'=4,'narrow'=4] {'wide'}, dimensions={0} | all-to-all | bytes 4194304 | tf_op jit(solution)/shard_map/all_to_all | solution.py:102
  247.1 25.5 %collective-permute-done = bf16[4,8,1,8,4096]{4,3,1,0,2:T(8,128)(2,1)S(1)} collective-permute-done((bf16[4,8,1,8,4096]{4,3,1,0,2:T(8,128)(2,1)S(1)}, bf16[4,8,1,8,4096]{4,3,1,0,2:T(8,128)(2,1)S(1)}, u32[]{:S(2)}, u32[]{:S(2)}) %collective-permute-start) | collective-permute-done | bytes 2097184 | tf_op jit(solution)/shard_map/ppermute | solution.py:114
  272.6 25.5 %collective-permute-done.1 = bf16[4,8,1,8,4096]{4,3,1,0,2:T(8,128)(2,1)S(1)} collective-permute-done((bf16[4,8,1,8,4096]{4,3,1,0,2:T(8,128)(2,1)S(1)}, bf16[4,8,1,8,4096]{4,3,1,0,2:T(8,128)(2,1)S(1)}, u32[]{:S(2)}, u32[]{:S(2)}) %collective-permute-start.1) | collective-permute-done | bytes 2097184 | tf_op jit(solution)/shard_map/ppermute | solution.py:114
  298.1 25.4 %collective-permute-done.2 = bf16[4,8,1,8,4096]{4,3,1,0,2:T(8,128)(2,1)S(1)} collective-permute-done((bf16[4,8,1,8,4096]{4,3,1,0,2:T(8,128)(2,1)S(1)}, bf16[4,8,1,8,4096]{4,3,1,0,2:T(8,128)(2,1)S(1)}, u32[]{:S(2)}, u32[]{:S(2)}) %collective-permute-start.2) | collective-permute-done | bytes 2097184 | tf_op jit(solution)/shard_map/ppermute | solution.py:114
  323.5 1.1 pad_maximum_fusion
  324.6 3.8 slice_bitcast_fusion.1
  328.5 4.9 %gather_fusion.2 = bf16[4,4,8,8,2048]{4,3,2,1,0:T(8,128)(2,1)} fusion(bf16[4,4,8,8,2048]{4,3,2,1,0:T(8,128)(2,1)} %get-tuple-element.7, s32[1024]{0:T(1024)S(1)} %pad_clamp_fusion.1), kind=kCustom, calls=%fused_computation.2 | custom fusion | bytes 8388624 | tf_op jit(solution)/shard_map/gather | solution.py:116
  333.4 5.0 %gather_fusion.3 = bf16[4,4,8,8,2048]{4,3,2,1,0:T(8,128)(2,1)} fusion(bf16[4,4,8,8,2048]{4,3,2,1,0:T(8,128)(2,1)} %get-tuple-element.8, s32[1024]{0:T(1024)S(1)} %pad_clamp_fusion.1), kind=kCustom, calls=%fused_computation.3 | custom fusion | bytes 8388624 | tf_op jit(solution)/shard_map/gather | solution.py:116
  338.4 12.6 %fusion.13 = f32[4,8,32,256]{3,2,0,1:T(8,128)S(1)} fusion(bf16[8,4096,256]{2,1,0:T(8,128)(2,1)} %param.20, bf16[4,4,8,1,8,2048]{5,4,2,1,0,3:T(8,128)(2,1)} %bitcast.136, bf16[4,4,8,1,8,2048]{5,4,2,1,0,3:T(8,128)(2,1)} %bitcast.134), kind=kOutput, calls=%fused_computation.23 | convolution fusion | flops 2164260864 | bytes 26214400 | tf_op jit(solution)/shard_map/wesd,edh->wesh/dot_general | solution.py:119
  351.0 13.5 %fusion.28 = bf16[4,8,32,256]{3,2,0,1:T(8,128)(2,1)} fusion(bf16[8,4096,256]{2,1,0:T(8,128)(2,1)} %param.21, f32[4,8,32,256]{3,2,0,1:T(8,128)S(1)} %fusion.13, bf16[4,4,8,1,8,2048]{5,4,2,1,0,3:T(8,128)(2,1)} %bitcast.137, bf16[4,4,8,1,8,2048]{5,4,2,1,0,3:T(8,128)(2,1)} %bitcast.135), kind=kOutput, calls=%fused_computation.26 | convolution fusion | flops 2165833728 | bytes 26738688 | tf_op jit(solution)/shard_map/wesd,edh->wesh/dot_general | solution.py:120
  364.5 21.1 %all-gather.5.cloned.1.call-done = bf16[4,8,32,1024]{3,2,0,1:T(8,128)(2,1)} async-done(((bf16[4,8,32,256]{3,2,0,1:T(8,128)(2,1)}), bf16[4,8,32,1024]{3,2,0,1:T(8,128)(2,1)}) %all-gather.5.cloned.1.call-update) | async-done | bytes 2097168 | tf_op jit(solution)/shard_map/all_gather | solution.py:125
  385.7 8.8 %convert_bitcast_fusion = bf16[4,8,4,8,1024]{4,3,2,0,1:T(8,128)(2,1)S(1)} fusion(bf16[4,8,32,1024]{3,2,0,1:T(8,128)(2,1)} %all-gather.5.cloned.1.call-done, bf16[8,1024,1024]{2,1,0:T(8,128)(2,1)} %param.22), kind=kOutput, calls=%fused_computation.21 | convolution fusion | flops 2148532224 | bytes 20971520 | tf_op jit(solution)/shard_map/wesh,ehd->wesd/dot_general | solution.py:123
  394.4 0.2 copy.42
  394.6 53.0 %all_to_all.26 = bf16[4,8,4,8,1024]{4,3,2,1,0:T(8,128)(2,1)S(1)} all-to-all(bf16[4,8,4,8,1024]{4,3,2,1,0:T(8,128)(2,1)S(1)} %copy.42), channel_id=1, replica_groups=mesh['groups'=2,'wide'=4,'narrow'=4] {'wide'}, dimensions={0} | all-to-all | bytes 4194304 | tf_op jit(solution)/shard_map/all_to_all | solution.py:131
  447.6 1.5 copy.43
  449.2 3.6 all-to-all-start.2
  452.8 0.1 reshape.189
  452.9 0.1 constant_dynamic-slice_fusion.1
  452.9 0.1 copy.37
  453.0 25.4 %all-to-all-done.2 = bf16[4,8,4,8,1024]{4,3,0,1,2:T(8,128)(2,1)S(1)} async-done(((bf16[4,8,4,8,1024]{4,3,0,1,2:T(8,128)(2,1)}), bf16[4,8,4,8,1024]{4,3,0,1,2:T(8,128)(2,1)S(1)}, u32[]{:S(2)}, u32[]{:S(2)}) %all-to-all-start.2) | async-done | bytes 2097184 | tf_op jit(solution)/shard_map/all_to_all | solution.py:130
  478.4 1.3 copy-done.2
  479.8 1.8 copy.44
  481.6 1.2 gather_fusion.1
  482.8 0.8 fusion.10
  483.6 1.2 multiply_reduce_fusion
  484.8 0.5 broadcast_multiply_fusion
  (34 shorter events, 0.3 us)
Async XLA Ops:
  6.5 2.8 copy-start
  6.5 154.7 %all-gather.3.cloned.1.call-start = ((), (), s32[]{:S(2)}) async-start(), calls=%async_computation.4 | async-start | bytes 10485760 | tf_op jit(solution)/shard_map/all_gather | solution.py:89
  7.3 183.2 %reduce-scatter.2.cloned.1.call-start = ((), (), s32[]{:S(2)}) async-start(), calls=%async_computation.5 | async-start | bytes 1310720 | tf_op jit(solution)/shard_map/reduce_scatter | solution.py:94
  9.6 157.7 %copy-start.6 = (s32[64,8]{0,1:T(8,128)S(1)}, s32[64,8]{0,1:T(8,128)}, u32[]{:S(2)}) copy-start(s32[64,8]{0,1:T(8,128)} %param.23) | copy-start | bytes 6148
  9.6 180.8 %copy-start.4 = (bf16[64,4096]{1,0:T(8,128)(2,1)S(1)}, bf16[64,4096]{1,0:T(8,128)(2,1)}, u32[]{:S(2)}) copy-start(bf16[64,4096]{1,0:T(8,128)(2,1)} %param.13) | copy-start | bytes 1572868
  9.7 181.9 %copy-start.5 = (f32[4096]{0:T(1024)S(1)}, f32[4096]{0:T(1024)}, u32[]{:S(2)}) copy-start(f32[4096]{0:T(1024)} %param.19) | copy-start | bytes 49156
  167.3 218.3 %all-gather.5.cloned.1.call-start = ((), (), s32[]{:S(2)}) async-start(), calls=%async_computation.6 | async-start | bytes 2621440 | tf_op jit(solution)/shard_map/all_gather | solution.py:125
  247.1 25.5 %collective-permute-start = (bf16[4,8,1,8,4096]{4,3,1,0,2:T(8,128)(2,1)S(1)}, bf16[4,8,1,8,4096]{4,3,1,0,2:T(8,128)(2,1)S(1)}, u32[]{:S(2)}, u32[]{:S(2)}) collective-permute-start(bf16[4,8,1,8,4096]{4,3,1,0,2:T(8,128)(2,1)S(1)} %bitcast.132), channel_id=1, source_target_pairs={{0,1},{1,2},{2,3},{3,0},{4,5},{5,6},{6,7},{7,4},{8,9},{9,10},{10,1... | collective-permute-start | bytes 6291464 | tf_op jit(solution)/shard_map/ppermute | solution.py:114
  272.6 25.5 %collective-permute-start.1 = (bf16[4,8,1,8,4096]{4,3,1,0,2:T(8,128)(2,1)S(1)}, bf16[4,8,1,8,4096]{4,3,1,0,2:T(8,128)(2,1)S(1)}, u32[]{:S(2)}, u32[]{:S(2)}) collective-permute-start(bf16[4,8,1,8,4096]{4,3,1,0,2:T(8,128)(2,1)S(1)} %collective-permute-done), channel_id=1, source_target_pairs={{0,1},{1,2},{2,3},{3,0},{4,5},{5,6},{6,7},{7,4},{8,9},{9,10},{10,1... | collective-permute-start | bytes 6291464 | tf_op jit(solution)/shard_map/ppermute | solution.py:114
  298.1 25.5 %collective-permute-start.2 = (bf16[4,8,1,8,4096]{4,3,1,0,2:T(8,128)(2,1)S(1)}, bf16[4,8,1,8,4096]{4,3,1,0,2:T(8,128)(2,1)S(1)}, u32[]{:S(2)}, u32[]{:S(2)}) collective-permute-start(bf16[4,8,1,8,4096]{4,3,1,0,2:T(8,128)(2,1)S(1)} %collective-permute-done.1), channel_id=1, source_target_pairs={{0,1},{1,2},{2,3},{3,0},{4,5},{5,6},{6,7},{7,4},{8,9},{9,10},{10,1... | collective-permute-start | bytes 6291464 | tf_op jit(solution)/shard_map/ppermute | solution.py:114
  447.6 5.2 %copy-start.7 = (f32[64,8]{0,1:T(8,128)S(1)}, f32[64,8]{0,1:T(8,128)}, u32[]{:S(2)}) copy-start(f32[64,8]{0,1:T(8,128)} %param.24) | copy-start | bytes 6148
  449.2 29.2 %all-to-all-start.2 = ((bf16[4,8,4,8,1024]{4,3,0,1,2:T(8,128)(2,1)}), bf16[4,8,4,8,1024]{4,3,0,1,2:T(8,128)(2,1)S(1)}, u32[]{:S(2)}, u32[]{:S(2)}) async-start(bf16[4,8,4,8,1024]{4,3,0,1,2:T(8,128)(2,1)} %copy.43), calls=%async_computation.3 | async-start | bytes 4194304 | tf_op jit(solution)/shard_map/all_to_all | solution.py:130
  478.4 1.4 copy-start.2
  481.6 3.7 copy-start.1
  481.6 2.0 copy-start.3
Sparse Core Ops, SparseCore 0:
  8.9 152.3 all-gather.2
  167.4 22.9 reduce-scatter.1
  364.7 20.9 all-gather.4
